TPU v7x, 32 devices: a whole 2x2x4 slice. The times are simulated.
32 devices in a mesh: wide: 8 (over z, core), narrow: 4 (over y, x).
Axes of the slice: x: 2, y: 2, z: 4, core: 2. Of those that a mesh axis runs over, the one named last changes fastest.
Arguments:
- tokens: bfloat16 [4096, 2048], P('wide'), may hold values from -6 to 6
- attn_gain: bfloat16 [2048], replicated, may hold values from 0.099609375 to 1.8984375
- w_query: bfloat16 [2048, 2048], P(None, 'narrow'), may hold values from -0.125 to 0.125
- w_key: bfloat16 [2048, 512], P(None, 'narrow'), may hold values from -0.125 to 0.125
- w_value: bfloat16 [2048, 512], P(None, 'narrow'), may hold values from -0.125 to 0.125
- w_out: bfloat16 [2048, 2048], P('narrow'), may hold values from -2 to 2
- ffn_gain: bfloat16 [2048], replicated, may hold values from 0.099609375 to 1.8984375
- w_gate: bfloat16 [2048, 8192], P(None, 'narrow'), may hold values from -0.125 to 0.125
- w_up: bfloat16 [2048, 8192], P(None, 'narrow'), may hold values from -0.125 to 0.125
- w_down: bfloat16 [8192, 2048], P('narrow'), may hold values from -0.0625 to 0.0625
- doc_lengths: int32 [12], replicated, may hold values from 1 to 2048, 4096 in all
- cotangent: bfloat16 [4096, 2048], P('wide'), may hold values from -6 to 6
Outputs:
- output: bfloat16 [4096, 2048], P('wide')
- input_grad: bfloat16 [4096, 2048], P('wide')
- grad_attn_gain: float32 [2048], P('wide')
- grad_query: float32 [2048, 2048], P('wide', 'narrow')
- grad_key: float32 [2048, 512], P('wide', 'narrow')
- grad_value: float32 [2048, 512], P('wide', 'narrow')
- grad_out: float32 [2048, 2048], P('narrow', 'wide')
- grad_ffn_gain: float32 [2048], P('wide')
- grad_gate: float32 [2048, 8192], P('wide', 'narrow')
- grad_up: float32 [2048, 8192], P('wide', 'narrow')
- grad_down: float32 [8192, 2048], P('narrow', 'wide')
Inputs may be any that keep to these rules, and one draw needn't show every extreme that they name: `doc_lengths`: the last entry is the padding at the row's end; the longest entry is exactly 2048.
All inputs are finite; a program needn't handle non-finite values.
Results may differ from a plain program's by a relative error of at most 0.02.
Values may be sent and summed in bfloat16 or wider, within the bound.
No kernel may reach another device: no remote copies, remote signals or barrier semaphores. Data moves between devices by JAX's collectives and lax.ppermute only.
A program may use at most 320 MiB of HBM per device.

v0:
```python
import math
import jax
import jax.numpy as jnp
import numpy as np
from jax import lax
from jax.sharding import PartitionSpec as P

HD = 64
QBLK = 512
DOCS = 12
NORM_EPS = 1e-05
MASKED_SCORE = -1e30


def inverse_frequencies(head_size):
    frequency = 1.0 / 500000.0 ** (np.arange(0, head_size, 2) / head_size)
    wavelength = 2 * math.pi / frequency
    smoothing = (8192.0 / wavelength - 1.0) / 3.0
    scaled_freq = np.where(wavelength > 8192.0, frequency / 32.0, frequency)
    middle_band = (wavelength <= 8192.0) & (wavelength >= 2048.0)
    scaled_freq = np.where(
        middle_band, (1 - smoothing) * frequency / 32.0 + smoothing * frequency, scaled_freq
    )
    return scaled_freq.astype(np.float32)


def doc_layout(doc_lengths, index):
    ends = jnp.cumsum(doc_lengths)
    passed = (index[:, None] >= ends[None, :]).astype(jnp.int32)
    segment = jnp.sum(passed, axis=1)
    offset = jnp.sum(passed * doc_lengths[None, :], axis=1)
    position = index - offset
    valid = index < ends[DOCS - 2]
    return (segment, position, valid)


def rotate(values, position, heads, direction):
    angle = position.astype(jnp.float32)[:, None] * jnp.asarray(inverse_frequencies(HD))[None, :]
    cosine = jnp.cos(angle)[:, None, :]
    sine = direction * jnp.sin(angle)[:, None, :]
    shaped = values.reshape(values.shape[0], heads, 2, HD // 2)
    first = shaped[:, :, 0]
    second = shaped[:, :, 1]
    return jnp.stack(
        [first * cosine - second * sine, second * cosine + first * sine], axis=2
    ).reshape(values.shape)


def contract_rows(left, right):
    return lax.dot_general(
        left, right, (((0,), (0,)), ((), ())), preferred_element_type=jnp.float32
    )


def contract_cols(left, right):
    return lax.dot_general(
        left, right, (((1,), (1,)), ((), ())), preferred_element_type=jnp.float32
    )


def head_scores(query_head, key_head, allowed):
    raw_scores = contract_cols(query_head, key_head)
    return jnp.where(allowed, raw_scores / math.sqrt(HD), MASKED_SCORE)


def norm_back(grad_normed, gain, values, inverse):
    scaled = grad_normed * gain
    return inverse * scaled - values * inverse**3 * jnp.mean(
        scaled * values, axis=-1, keepdims=True
    )


def body(
    tokens,
    attn_gain,
    w_query,
    w_key,
    w_value,
    w_out,
    ffn_gain,
    w_gate,
    w_up,
    w_down,
    doc_lengths,
    cotangent,
):
    rows = tokens.shape[0]
    total = rows * lax.axis_size("wide")
    heads = w_query.shape[1] // HD
    kv_heads = w_key.shape[1] // HD
    group = heads // kv_heads
    blocks = rows // QBLK
    local_index = lax.axis_index("wide") * rows + jnp.arange(rows, dtype=jnp.int32)
    segment, position, valid = doc_layout(doc_lengths, local_index)
    key_index = jnp.arange(total, dtype=jnp.int32)
    key_layout = doc_layout(doc_lengths, key_index)
    key_segment = key_layout[0]
    inputs = tokens.astype(jnp.float32)
    gain_one = attn_gain.astype(jnp.float32)
    gain_two = ffn_gain.astype(jnp.float32)
    inv_one = lax.rsqrt(jnp.mean(inputs * inputs, axis=-1, keepdims=True) + NORM_EPS)
    normed = (inputs * inv_one * gain_one).astype(jnp.bfloat16)
    query = jnp.dot(normed, w_query, preferred_element_type=jnp.float32)
    keys = jnp.dot(normed, w_key, preferred_element_type=jnp.float32)
    values = jnp.dot(normed, w_value, preferred_element_type=jnp.float32).astype(jnp.bfloat16)
    query_r = rotate(query, position, heads, 1.0).astype(jnp.bfloat16)
    keys_r = rotate(keys, position, kv_heads, 1.0).astype(jnp.bfloat16)
    packed = jnp.concatenate([keys_r, values], axis=1)
    gathered = lax.all_gather(packed, "wide", axis=0, tiled=True)
    width = kv_heads * HD
    all_keys = gathered[:, :width]
    all_values = gathered[:, width:]

    def block_mask(segment_block, index_block):
        return (segment_block[:, None] == key_segment[None, :]) & (
            index_block[:, None] >= key_index[None, :]
        )

    def attend(block_in):
        query_block, segment_block, index_block = block_in
        allowed = block_mask(segment_block, index_block)
        outputs = []
        totals = []
        for head in range(heads):
            column = head // group * HD
            scores = head_scores(
                query_block[:, head * HD : (head + 1) * HD],
                all_keys[:, column : column + HD],
                allowed,
            )
            row_max = jnp.max(scores, axis=1, keepdims=True)
            exponent = jnp.exp(scores - row_max)
            row_sum = jnp.sum(exponent, axis=1, keepdims=True)
            probs = (exponent / row_sum).astype(jnp.bfloat16)
            outputs.append(
                jnp.dot(
                    probs, all_values[:, column : column + HD], preferred_element_type=jnp.float32
                )
            )
            totals.append(row_max[:, 0] + jnp.log(row_sum[:, 0]))
        return (jnp.concatenate(outputs, axis=1), jnp.stack(totals, axis=1))

    query_blocks = query_r.reshape(blocks, QBLK, heads * HD)
    segment_blocks = segment.reshape(blocks, QBLK)
    index_blocks = local_index.reshape(blocks, QBLK)
    attended, log_sums = lax.map(attend, (query_blocks, segment_blocks, index_blocks))
    valid_rows = valid[:, None]
    mixed = jnp.where(valid_rows, attended.reshape(rows, heads * HD), 0.0).astype(jnp.bfloat16)
    attn_part = jnp.dot(mixed, w_out, preferred_element_type=jnp.float32)
    hidden_one = inputs + lax.psum(attn_part, "narrow")
    inv_two = lax.rsqrt(jnp.mean(hidden_one * hidden_one, axis=-1, keepdims=True) + NORM_EPS)
    normed_two = (hidden_one * inv_two * gain_two).astype(jnp.bfloat16)
    gate = jnp.dot(normed_two, w_gate, preferred_element_type=jnp.float32)
    up_proj = jnp.dot(normed_two, w_up, preferred_element_type=jnp.float32)
    sigmoid_gate = jax.nn.sigmoid(gate)
    silu_gate = gate * sigmoid_gate
    activ = (silu_gate * up_proj).astype(jnp.bfloat16)
    ffn_part = jnp.dot(activ, w_down, preferred_element_type=jnp.float32)
    grad_down = contract_rows(activ, cotangent)
    d_activ = contract_cols(cotangent, w_down)
    d_gate = (d_activ * up_proj * sigmoid_gate * (1.0 + gate * (1.0 - sigmoid_gate))).astype(
        jnp.bfloat16
    )
    d_up = (d_activ * silu_gate).astype(jnp.bfloat16)
    grad_gate = contract_rows(normed_two, d_gate)
    grad_up = contract_rows(normed_two, d_up)
    norm_two_part = contract_cols(d_gate, w_gate) + contract_cols(d_up, w_up)
    output = (
        hidden_one + lax.psum(ffn_part.astype(jnp.bfloat16), "narrow").astype(jnp.float32)
    ).astype(jnp.bfloat16)
    d_norm_two = lax.psum(norm_two_part.astype(jnp.bfloat16), "narrow").astype(jnp.float32)
    grad_ffn_gain = jnp.sum(d_norm_two * hidden_one * inv_two, axis=0)
    d_hidden = cotangent.astype(jnp.float32) + norm_back(d_norm_two, gain_two, hidden_one, inv_two)
    d_hidden_b = d_hidden.astype(jnp.bfloat16)
    grad_out = contract_rows(mixed, d_hidden_b)
    d_mixed = jnp.where(
        valid_rows,
        contract_cols(d_hidden_b, w_out).astype(jnp.bfloat16),
        jnp.zeros((), jnp.bfloat16),
    )

    def attend_back(carry, block_in):
        query_block, grad_block, lse_block, segment_block, index_block = block_in
        allowed = block_mask(segment_block, index_block)
        query_grads = []
        key_terms = [None] * kv_heads
        value_terms = [None] * kv_heads
        for head in range(heads):
            kv_index = head // group
            column = kv_index * HD
            query_head = query_block[:, head * HD : (head + 1) * HD]
            grad_head = grad_block[:, head * HD : (head + 1) * HD]
            key_head = all_keys[:, column : column + HD]
            value_head = all_values[:, column : column + HD]
            scores = head_scores(query_head, key_head, allowed)
            probs = jnp.where(allowed, jnp.exp(scores - lse_block[:, head : head + 1]), 0.0)
            prob_grad = contract_cols(grad_head, value_head)
            delta = jnp.sum(probs * prob_grad, axis=1, keepdims=True)
            d_scores = (probs * (prob_grad - delta)).astype(jnp.bfloat16)
            query_grads.append(
                jnp.dot(d_scores, key_head, preferred_element_type=jnp.float32) / math.sqrt(HD)
            )
            key_term = contract_rows(d_scores, query_head) / math.sqrt(HD)
            value_term = contract_rows(probs.astype(jnp.bfloat16), grad_head)
            if key_terms[kv_index] is None:
                key_terms[kv_index] = key_term
                value_terms[kv_index] = value_term
            else:
                key_terms[kv_index] = key_terms[kv_index] + key_term
                value_terms[kv_index] = value_terms[kv_index] + value_term
        update = jnp.concatenate(key_terms + value_terms, axis=1)
        return (carry + update, jnp.concatenate(query_grads, axis=1))

    start_terms = jnp.zeros((total, 2 * width), jnp.float32)
    grad_blocks = d_mixed.reshape(blocks, QBLK, heads * HD)
    kv_terms, query_grad_blocks = lax.scan(
        attend_back,
        start_terms,
        (query_blocks, grad_blocks, log_sums, segment_blocks, index_blocks),
    )
    d_kv = lax.psum_scatter(
        kv_terms.astype(jnp.bfloat16), "wide", scatter_dimension=0, tiled=True
    ).astype(jnp.float32)
    d_query = rotate(query_grad_blocks.reshape(rows, heads * HD), position, heads, -1.0).astype(
        jnp.bfloat16
    )
    d_keys = rotate(d_kv[:, :width], position, kv_heads, -1.0).astype(jnp.bfloat16)
    d_values = d_kv[:, width:].astype(jnp.bfloat16)
    grad_query = contract_rows(normed, d_query)
    grad_key = contract_rows(normed, d_keys)
    grad_value = contract_rows(normed, d_values)
    norm_one_part = (
        contract_cols(d_query, w_query)
        + contract_cols(d_keys, w_key)
        + contract_cols(d_values, w_value)
    )
    d_norm_one = lax.psum(norm_one_part.astype(jnp.bfloat16), "narrow").astype(jnp.float32)
    grad_attn_gain = jnp.sum(d_norm_one * inputs * inv_one, axis=0)
    input_grad = (d_hidden + norm_back(d_norm_one, gain_one, inputs, inv_one)).astype(jnp.bfloat16)
    summed = (
        lax.psum_scatter(
            grad_attn_gain.astype(jnp.bfloat16), "wide", scatter_dimension=0, tiled=True
        ).astype(jnp.float32),
        lax.psum_scatter(
            grad_query.astype(jnp.bfloat16), "wide", scatter_dimension=0, tiled=True
        ).astype(jnp.float32),
        lax.psum_scatter(
            grad_key.astype(jnp.bfloat16), "wide", scatter_dimension=0, tiled=True
        ).astype(jnp.float32),
        lax.psum_scatter(
            grad_value.astype(jnp.bfloat16), "wide", scatter_dimension=0, tiled=True
        ).astype(jnp.float32),
        lax.psum_scatter(
            grad_out.astype(jnp.bfloat16), "wide", scatter_dimension=1, tiled=True
        ).astype(jnp.float32),
        lax.psum_scatter(
            grad_ffn_gain.astype(jnp.bfloat16), "wide", scatter_dimension=0, tiled=True
        ).astype(jnp.float32),
        lax.psum_scatter(
            grad_gate.astype(jnp.bfloat16), "wide", scatter_dimension=0, tiled=True
        ).astype(jnp.float32),
        lax.psum_scatter(
            grad_up.astype(jnp.bfloat16), "wide", scatter_dimension=0, tiled=True
        ).astype(jnp.float32),
        lax.psum_scatter(
            grad_down.astype(jnp.bfloat16), "wide", scatter_dimension=1, tiled=True
        ).astype(jnp.float32),
    )
    gain_attn = summed[0]
    gain_ffn = summed[5]
    return (
        output,
        input_grad,
        gain_attn,
        summed[1],
        summed[2],
        summed[3],
        summed[4],
        gain_ffn,
        summed[6],
        summed[7],
        summed[8],
    )


def solution(mesh):
    in_specs = (
        P("wide", None),
        P(),
        P(None, "narrow"),
        P(None, "narrow"),
        P(None, "narrow"),
        P("narrow", None),
        P(),
        P(None, "narrow"),
        P(None, "narrow"),
        P("narrow", None),
        P(),
        P("wide", None),
    )
    out_specs = (
        P("wide", None),
        P("wide", None),
        P("wide"),
        P("wide", "narrow"),
        P("wide", "narrow"),
        P("wide", "narrow"),
        P("narrow", "wide"),
        P("wide"),
        P("wide", "narrow"),
        P("wide", "narrow"),
        P("narrow", "wide"),
    )
    return jax.shard_map(body, mesh=mesh, in_specs=in_specs, out_specs=out_specs, check_vma=False)
```

profile of v0, /device:TPU:0, one launch (start us, length us, event | category | flops | bytes accessed | tf_op | source)
XLA Modules:
  0.0 1095.4 jit_solution(12022537940424208202)
XLA Ops:
  24.1 25.7 %all-gather.2.cloned.1.call-done = bf16[4096,256]{0,1:T(8,128)(2,1)} async-done(((bf16[512,256]{0,1:T(8,128)(2,1)}), bf16[4096,256]{0,1:T(8,128)(2,1)}) %all-gather.2.cloned.1.call-update) | async-done | bytes 2097168 | tf_op jit(solution)/shard_map/all_gather | solution.py:109
  96.0 7.2 fusion.169
  103.1 4.8 fusion.1
  107.9 5.0 fusion.60
  116.7 5.4 fusion.57
  134.7 103.2 %all-reduce.8.cloned.1.call-done = f32[512,2048]{1,0:T(8,128)} async-done(((f32[512,2048]{1,0:T(8,128)}), f32[512,2048]{1,0:T(8,128)}) %all-reduce.8.cloned.1.call-update) | async-done | bytes 4194320 | tf_op jit(solution)/shard_map/psum | solution.py:150
  241.9 9.3 fusion.178
  251.2 6.3 fusion.177
  257.5 12.0 %multiply_convert_fusion.8 = (bf16[512,2048]{1,0:T(8,128)(2,1)}, bf16[512,2048]{1,0:T(8,128)(2,1)}, bf16[512,2048]{1,0:T(8,128)(2,1)}) fusion(f32[512,2048]{1,0:T(8,128)} %fusion.177, f32[512,2048]{1,0:T(8,128)S(1)} %fusion.178, bf16[512,2048]{1,0:T(8,128)(2,1)S(1)} %copy-done.36, bf16[2048,2048]{1,0:T(8,128)(2,1)} %param.25), kind=kOutput, calls=%fused_computation.118 | convolution fusion | flops 4310695936 | bytes 25165824 | tf_op jit(solution)/shard_map/dot_general | solution.py:56
  269.5 7.8 fusion.179
  277.3 9.4 add_convert_fusion.1
  287.2 69.3 %all-reduce.10.cloned.1.call-done = bf16[512,2048]{1,0:T(8,128)(2,1)} async-done(((bf16[512,2048]{1,0:T(8,128)(2,1)}), bf16[512,2048]{1,0:T(8,128)(2,1)}) %all-reduce.10.cloned.1.call-update) | async-done | bytes 2097168 | tf_op jit(solution)/shard_map/psum | solution.py:171
  356.5 4.9 fusion.25
  399.6 4.9 fusion.94
  415.0 26.5 %multiply_reduce_fusion = (f32[512]{0:T(512)S(1)}, f32[512]{0:T(512)S(1)}, f32[512]{0:T(512)S(1)}, f32[512]{0:T(512)S(1)}, f32[512]{0:T(512)S(1)}, /*index=5*/f32[512,4096]{1,0:T(8,128)}) fusion(f32[512,4096]{1,0:T(8,128)} %copy-done.7, f32[512]{0:T(512)S(1)} %log_add_fusion, s32[512]{0:T(512)S(1)} %iota_add_fusion, s32[4096]{0:T(1024)S(1)} %convert_reduce_fusion, ...), kind=kOutput, calls=%fused_computation.7 | convolution fusion | flops 316667392 | bytes 84516864 | tf_op jit(solution)/shard_map/while/body/eval_jaxpr/dot_general | solution.py:56
  441.5 25.5 %multiply_reduce_fusion.1 = (f32[512]{0:T(512)S(1)}, f32[512]{0:T(512)S(1)}, f32[512]{0:T(512)S(1)}, bf16[512,4096]{1,0:T(8,128)(2,1)}, f32[512,4096]{1,0:T(8,128)}) fusion(f32[512,4096]{1,0:T(8,128)} %copy-done.4, f32[512]{0:T(512)S(1)} %get-tuple-element.145, s32[512]{0:T(512)S(1)} %iota_add_fusion, s32[4096]{0:T(1024)S(1)} %convert_reduce_fusion, ...), kind=kOutput, calls=%fused_computation.10 | convolution fusion | flops 310376960 | bytes 71929856 | tf_op jit(solution)/shard_map/while/body/eval_jaxpr/dot_general | solution.py:56
  467.0 21.2 %multiply_convert_fusion.2 = (bf16[512,4096]{1,0:T(8,128)(2,1)}, bf16[512,4096]{1,0:T(8,128)(2,1)}, bf16[512,4096]{1,0:T(8,128)(2,1)S(1)}) fusion(f32[512,4096]{1,0:T(8,128)} %fusion.78, f32[512]{0:T(512)S(1)} %get-tuple-element.88, f32[512,4096]{1,0:T(8,128)} %copy-done.8, f32[512]{0:T(512)S(1)} %get-tuple-element.146, s32[512]{0:T(512)S(1)} %iota_add_fusion, ...), kind=kLoop, calls=%fused_computation.12 | loop fusion | flops 37748736 | bytes 62947328 | tf_op jit(solution)/shard_map/while/body/eval_jaxpr/convert_element_type | solution.py:199
  492.1 27.0 %multiply_convert_fusion.1 = (bf16[512,4096]{1,0:T(8,128)(2,1)}, bf16[512,4096]{1,0:T(8,128)(2,1)}, bf16[512,4096]{1,0:T(8,128)(2,1)}, bf16[512,4096]{1,0:T(8,128)(2,1)}) fusion(f32[512,4096]{1,0:T(8,128)} %get-tuple-element.140, f32[512]{0:T(512)S(1)} %get-tuple-element.74, f32[512,4096]{1,0:T(8,128)} %copy-done.4, f32[512]{0:T(512)S(1)} %get-tuple-element.145, ...), kind=kLoop, calls=%fused_computation.9 | loop fusion | flops 48234496 | bytes 83922944 | tf_op jit(solution)/shard_map/while/body/eval_jaxpr/convert_element_type | solution.py:199
  558.0 11.5 %reduce-scatter.9.cloned.1.call-done = bf16[512,256]{0,1:T(8,128)(2,1)} async-done(((bf16[4096,256]{0,1:T(8,128)(2,1)}), bf16[512,256]{0,1:T(8,128)(2,1)}) %reduce-scatter.9.cloned.1.call-update) | async-done | bytes 262160 | tf_op jit(solution)/shard_map/reduce_scatter | solution.py:221
  572.8 10.0 convolution_convert_fusion.5
  591.0 10.1 convolution_convert_fusion.1
  601.3 10.1 convolution_convert_fusion.2
  611.4 10.3 convolution_convert_fusion
  625.4 17.5 %reduce-scatter.11.cloned.1.call-done = bf16[256,512]{1,0:T(8,128)(2,1)} async-done(((bf16[2048,512]{1,0:T(8,128)(2,1)}), bf16[256,512]{1,0:T(8,128)(2,1)}) %reduce-scatter.11.cloned.1.call-update) | async-done | bytes 262160 | tf_op jit(solution)/shard_map/reduce_scatter | solution.py:244
  644.7 30.1 %reduce-scatter.13.cloned.1.call-done = bf16[256,128]{1,0:T(8,128)(2,1)} async-done(((bf16[2048,128]{1,0:T(8,128)(2,1)}), bf16[256,128]{1,0:T(8,128)(2,1)}) %reduce-scatter.13.cloned.1.call-update) | async-done | bytes 65552 | tf_op jit(solution)/shard_map/reduce_scatter | solution.py:247
  676.2 30.1 %reduce-scatter.15.cloned.1.call-done = bf16[256,128]{1,0:T(8,128)(2,1)} async-done(((bf16[2048,128]{1,0:T(8,128)(2,1)}), bf16[256,128]{1,0:T(8,128)(2,1)}) %reduce-scatter.15.cloned.1.call-update) | async-done | bytes 65552 | tf_op jit(solution)/shard_map/reduce_scatter | solution.py:250
  707.8 105.0 %all-reduce.12.cloned.1.call-done = (bf16[512,2048]{1,0:T(8,128)(2,1)}, bf16[512,2048]{1,0:T(8,128)(2,1)}) async-done(((bf16[512,2048]{1,0:T(8,128)(2,1)}, bf16[512,2048]{1,0:T(8,128)(2,1)}), (bf16[512,2048]{1,0:T(8,128)(2,1)}, bf16[512,2048]{1,0:T(8,128)(2,1)})) %all-reduce.12.cloned.1.call-update) | async-done | bytes 4194320 | tf_op jit(solution)/shard_map/psum | solution.py:169
  816.0 17.4 %all-reduce.2 = (bf16[2048]{0:T(1024)(128)(2,1)S(1)}, bf16[2048]{0:T(1024)(128)(2,1)S(1)}) all-reduce(bf16[2048]{0:T(1024)(128)(2,1)S(1)} %get-tuple-element.67, bf16[2048]{0:T(1024)(128)(2,1)S(1)} %copy-done.52), channel_id=3, replica_groups=mesh['wide'=8,'narrow'=4] {'wide'}, use_global_device_ids=true, to_apply=%region_38.39.clone | all-reduce | flops 4096 | bytes 16384
  834.7 5.1 add_convert_fusion.2
  843.5 61.7 %reduce-scatter.21.cloned.1.call-done = bf16[256,2048]{1,0:T(8,128)(2,1)} async-done(((bf16[2048,2048]{1,0:T(8,128)(2,1)}), bf16[256,2048]{1,0:T(8,128)(2,1)}) %reduce-scatter.21.cloned.1.call-update) | async-done | bytes 1048592 | tf_op jit(solution)/shard_map/reduce_scatter | solution.py:262
  908.0 87.4 %reduce-scatter.19.cloned.1.call-done = bf16[256,2048]{1,0:T(8,128)(2,1)} async-done(((bf16[2048,2048]{1,0:T(8,128)(2,1)}), bf16[256,2048]{1,0:T(8,128)(2,1)}) %reduce-scatter.19.cloned.1.call-update) | async-done | bytes 1048592 | tf_op jit(solution)/shard_map/reduce_scatter | solution.py:259
  998.2 87.4 %reduce-scatter.23.cloned.1.call-done = bf16[2048,256]{1,0:T(8,128)(2,1)} async-done(((bf16[2048,2048]{1,0:T(8,128)(2,1)}), bf16[2048,256]{1,0:T(8,128)(2,1)}) %reduce-scatter.23.cloned.1.call-update) | async-done | bytes 1048592 | tf_op jit(solution)/shard_map/reduce_scatter | solution.py:265
  (313 shorter events, 210.1 us)
Async XLA Ops:
  7.2 123.9 %copy-start = (bf16[512,2048]{1,0:T(8,128)(2,1)S(1)}, bf16[512,2048]{1,0:T(8,128)(2,1)}, u32[]{:S(2)}) copy-start(bf16[512,2048]{1,0:T(8,128)(2,1)} %param.21) | copy-start | bytes 6291460
  7.2 7.9 copy-start.40
  7.2 42.6 %all-gather.2.cloned.1.call-start = ((), (), s32[]{:S(2)}) async-start(), calls=%async_computation.8 | async-start | bytes 2359296 | tf_op jit(solution)/shard_map/all_gather | solution.py:109
  10.1 9.4 copy-start.50
  17.9 220.0 %all-reduce.8.cloned.1.call-start = ((), (), s32[]{:S(2)}) async-start(), calls=%async_computation.9 | async-start | bytes 8388608 | tf_op jit(solution)/shard_map/psum | solution.py:150
  19.3 345.7 %copy-start.53 = (pred[512]{0:T(512)(128)(4,1)}, pred[512]{0:T(512)(128)(4,1)S(1)}, u32[]{:S(2)}) copy-start(pred[512]{0:T(512)(128)(4,1)S(1)} %fusion.150) | copy-start | bytes 1540
  61.6 64.6 %copy-start.4 = (f32[512,4096]{1,0:T(8,128)}, f32[512,4096]{1,0:T(8,128)S(1)}, u32[]{:S(2)}) copy-start(f32[512,4096]{1,0:T(8,128)S(1)} %get-tuple-element.136) | copy-start | bytes 25165828
  88.9 25.9 %copy-start.5 = (f32[512,4096]{1,0:T(8,128)}, f32[512,4096]{1,0:T(8,128)S(1)}, u32[]{:S(2)}) copy-start(f32[512,4096]{1,0:T(8,128)S(1)} %get-tuple-element.128) | copy-start | bytes 25165828
  94.7 18.3 %copy-start.6 = (f32[512,4096]{1,0:T(8,128)}, f32[512,4096]{1,0:T(8,128)S(1)}, u32[]{:S(2)}) copy-start(f32[512,4096]{1,0:T(8,128)S(1)} %get-tuple-element.126) | copy-start | bytes 25165828
  134.4 222.1 %all-reduce.10.cloned.1.call-start = ((), (), s32[]{:S(2)}) async-start(), calls=%async_computation.10 | async-start | bytes 4194304 | tf_op jit(solution)/shard_map/psum | solution.py:171
  241.4 9.8 copy-start.2
  241.4 9.8 slice-start.22
  241.8 9.4 copy-start.35
  241.8 9.4 slice-start.23
  286.7 282.8 %reduce-scatter.9.cloned.1.call-start = ((), (), s32[]{:S(2)}) async-start(), calls=%async_computation.11 | async-start | bytes 2359296 | tf_op jit(solution)/shard_map/reduce_scatter | solution.py:221
  356.5 10.7 slice-start.14
  370.2 8.7 slice-start.20
  376.2 8.4 slice-start
  467.0 23.3 %copy-start.34 = (bf16[512,8,2,32]{0,3,2,1:T(8,128)(2,1)S(1)}, bf16[512,8,2,32]{0,3,2,1:T(8,128)(2,1)}, u32[]{:S(2)}) copy-start(bf16[512,8,2,32]{0,3,2,1:T(8,128)(2,1)} %pad_maximum_fusion.1) | copy-start | bytes 1572868
  533.5 90.1 %reduce-scatter.17.cloned.1.call-start = ((), (), s32[]{:S(2)}) async-start(), calls=%async_computation.15 | async-start | bytes 2359296 | tf_op jit(solution)/shard_map/reduce_scatter | solution.py:253
  538.4 104.5 %reduce-scatter.11.cloned.1.call-start = ((), (), s32[]{:S(2)}) async-start(), calls=%async_computation.12 | async-start | bytes 2359296 | tf_op jit(solution)/shard_map/reduce_scatter | solution.py:244
  555.0 15.5 %copy-start.28 = (bf16[512,2048]{1,0:T(8,128)(2,1)S(1)}, bf16[512,2048]{1,0:T(8,128)(2,1)}, u32[]{:S(2)}) copy-start(bf16[512,2048]{1,0:T(8,128)(2,1)} %param.16) | copy-start | bytes 6291460
  557.9 116.8 %reduce-scatter.13.cloned.1.call-start = ((), (), s32[]{:S(2)}) async-start(), calls=%async_computation.13 | async-start | bytes 589824 | tf_op jit(solution)/shard_map/reduce_scatter | solution.py:247
  572.4 133.9 %reduce-scatter.15.cloned.1.call-start = ((), (), s32[]{:S(2)}) async-start(), calls=%async_computation.14 | async-start | bytes 589824 | tf_op jit(solution)/shard_map/reduce_scatter | solution.py:250
  572.8 10.1 copy-start.47
  584.7 228.1 %all-reduce.12.cloned.1.call-start = ((), (), s32[]{:S(2)}) async-start(), calls=%async_computation.19 | async-start | bytes 8388608 | tf_op jit(solution)/shard_map/psum | solution.py:169
  590.9 314.3 %reduce-scatter.21.cloned.1.call-start = ((), (), s32[]{:S(2)}) async-start(), calls=%async_computation.17 | async-start | bytes 9437184 | tf_op jit(solution)/shard_map/reduce_scatter | solution.py:262
  601.1 394.3 %reduce-scatter.19.cloned.1.call-start = ((), (), s32[]{:S(2)}) async-start(), calls=%async_computation.16 | async-start | bytes 9437184 | tf_op jit(solution)/shard_map/reduce_scatter | solution.py:259
  611.4 474.3 %reduce-scatter.23.cloned.1.call-start = ((), (), s32[]{:S(2)}) async-start(), calls=%async_computation.18 | async-start | bytes 9437184 | tf_op jit(solution)/shard_map/reduce_scatter | solution.py:265
  621.7 194.2 %copy-start.52 = (bf16[2048]{0:T(1024)(128)(2,1)S(1)}, bf16[2048]{0:T(1024)(128)(2,1)}, u32[]{:S(2)}) copy-start(bf16[2048]{0:T(1024)(128)(2,1)} %get-tuple-element.65) | copy-start | bytes 12292
  642.9 196.9 %copy-start.55 = (f32[512]{0:T(512)S(1)}, f32[512]{0:T(512)}, u32[]{:S(2)}) copy-start(f32[512]{0:T(512)} %get-tuple-element.119) | copy-start | bytes 6148
  840.9 247.5 %copy-start.1 = (bf16[512,2048]{1,0:T(8,128)(2,1)S(1)}, bf16[512,2048]{1,0:T(8,128)(2,1)}, u32[]{:S(2)}) copy-start(bf16[512,2048]{1,0:T(8,128)(2,1)} %param.21) | copy-start | bytes 6291460
  (64 other events, 237.7 us)
Sparse Core Ops, SparseCore 0:
  18.0 31.7 all-gather.1
  134.5 103.3 all-reduce.7
  286.8 69.6 all-reduce.9
  533.6 35.8 reduce-scatter.8
  571.6 34.4 reduce-scatter.16
  608.3 34.5 reduce-scatter.10
  645.1 29.5 reduce-scatter.12
  677.1 29.1 reduce-scatter.14
  710.4 102.3 all-reduce.11
  815.0 90.1 reduce-scatter.20
  907.6 87.7 reduce-scatter.18
  997.7 87.9 reduce-scatter.22
where the time goes:
time: 1100 us
  waiting for transfers between devices  629 us (57%)
  matrix products  293 us (27%)
  other arithmetic  112 us (10%)
  local copies, waits for them, and re-layouts  25.3 us (2%)
  blocking collectives  17.4 us (2%)
  between operations  16.3 us (1%)
    dot_general x23, matrix products, contract_cols(): lax.dot_general(left, right, (((1,), (1,)), ((), ())), preferred_element_...  147 us
    psum x1, waiting for transfers between devices, body(): lax.psum(ffn_part.astype(jnp.bfloat16), 'narrow').astype(jnp.float32)  105 us
    psum x1, waiting for transfers between devices, body(): hidden_one = inputs + lax.psum(attn_part, 'narrow')  103 us
    reduce_scatter x1, waiting for transfers between devices, body(): lax.psum_scatter(grad_down.astype(jnp.bfloat16), 'wide', scatter_dimensio...  87.4 us
    reduce_scatter x1, waiting for transfers between devices, body(): lax.psum_scatter(grad_gate.astype(jnp.bfloat16), 'wide', scatter_dimensio...  87.4 us
    dot_general x23, matrix products, contract_rows(): lax.dot_general(left, right, (((0,), (0,)), ((), ())), preferred_element_...  73.2 us
    psum x1, waiting for transfers between devices, body(): lax.psum(norm_two_part.astype(jnp.bfloat16), 'narrow').astype(jnp.float32)  69.3 us
    reduce_scatter x1, waiting for transfers between devices, body(): lax.psum_scatter(grad_up.astype(jnp.bfloat16), 'wide', scatter_dimension=...  61.7 us
  transfers between devices with their start and end apart: 12, of which 11 were waited for; matrix products, arithmetic and copies ran while one was open for 10% of the time, Pallas kernels for 0%

commit v1 on v0

--- a/solution.py
+++ b/solution.py
@@ -106,7 +106,12 @@
     query_r = rotate(query, position, heads, 1.0).astype(jnp.bfloat16)
     keys_r = rotate(keys, position, kv_heads, 1.0).astype(jnp.bfloat16)
     packed = jnp.concatenate([keys_r, values], axis=1)
-    gathered = lax.all_gather(packed, "wide", axis=0, tiled=True)
+    ring = [packed]
+    for hop in range(7):
+        ring.append(lax.ppermute(ring[-1], "wide", [(dev, (dev + 1) % 8) for dev in range(8)]))
+    gathered = jnp.roll(
+        jnp.concatenate(ring[::-1], axis=0), (lax.axis_index("wide") + 1) * ring[0].shape[0], axis=0
+    )
     width = kv_heads * HD
     all_keys = gathered[:, :width]
     all_values = gathered[:, width:]

time: 1100 us -> 1140 us (1.036)
  waiting for transfers between devices: 629 us -> 651 us
  other arithmetic: 112 us -> 129 us
    ppermute x0 -> x7, waiting for transfers between devices: none -> 48.6 us  [body(): lax.ppermute(ring[-1], 'wide', [(dev, (dev + 1) % 8) for dev in range(8)])]
    all_gather x1 -> x0, waiting for transfers between devices: 25.7 us -> none  [body(): gathered = lax.all_gather(packed, 'wide', axis=0, tiled=True)]
    reduce_sum x8, other arithmetic: 13.9 us -> 30.4 us  [attend(): row_sum = jnp.sum(exponent, axis=1, keepdims=True)]
    unnamed x169 -> x207, local copies, waits for them, and re-layouts: 23.8 us -> 21 us
  transfers between devices with their start and end apart: 12 -> 18, of which waited for: 11 -> 17; matrix products, arithmetic and copies ran while one was open for 10% -> 9% of each run, Pallas kernels for 0% -> 0%
where the time goes in v1:
time: 1140 us; the launch traced here: 1130 us
  waiting for transfers between devices  651 us (57%)
  matrix products  294 us (26%)
  other arithmetic  129 us (11%)
  local copies, waits for them, and re-layouts  22.5 us (2%)
  blocking collectives  17.2 us (2%)
  between operations  16.4 us (1%)
    dot_general x23, matrix products, contract_cols(): lax.dot_general(left, right, (((1,), (1,)), ((), ())), preferred_element_...  151 us
    psum x1, waiting for transfers between devices, body(): lax.psum(ffn_part.astype(jnp.bfloat16), 'narrow').astype(jnp.float32)  105 us
    psum x1, waiting for transfers between devices, body(): hidden_one = inputs + lax.psum(attn_part, 'narrow')  103 us
    reduce_scatter x1, waiting for transfers between devices, body(): lax.psum_scatter(grad_down.astype(jnp.bfloat16), 'wide', scatter_dimensio...  87.6 us
    reduce_scatter x1, waiting for transfers between devices, body(): lax.psum_scatter(grad_gate.astype(jnp.bfloat16), 'wide', scatter_dimensio...  87.3 us
    dot_general x23, matrix products, contract_rows(): lax.dot_general(left, right, (((0,), (0,)), ((), ())), preferred_element_...  76 us
    psum x1, waiting for transfers between devices, body(): lax.psum(norm_two_part.astype(jnp.bfloat16), 'narrow').astype(jnp.float32)  69.4 us
    reduce_scatter x1, waiting for transfers between devices, body(): lax.psum_scatter(grad_up.astype(jnp.bfloat16), 'wide', scatter_dimension=...  62.1 us
  transfers between devices with their start and end apart: 18, of which 17 were waited for; matrix products, arithmetic and copies ran while one was open for 9% of the time, Pallas kernels for 0%

profile of v1, /device:TPU:0, one launch (start us, length us, event | category | flops | bytes accessed | tf_op | source)
XLA Modules:
  0.0 1133.2 jit_solution(17906079457685394254)
XLA Ops:
  17.9 8.1 collective-permute-done
  26.0 7.6 collective-permute-done.1
  33.6 7.6 collective-permute-done.2
  41.2 7.6 collective-permute-done.3
  48.8 7.6 collective-permute-done.4
  67.0 5.5 collective-permute-done.6
  110.2 7.7 fusion.6
  165.5 102.6 %all-reduce.8.cloned.1.call-done = f32[512,2048]{1,0:T(8,128)} async-done(((f32[512,2048]{1,0:T(8,128)}), f32[512,2048]{1,0:T(8,128)}) %all-reduce.8.cloned.1.call-update) | async-done | bytes 4194320 | tf_op jit(solution)/shard_map/psum | solution.py:155
  272.1 9.3 fusion.186
  281.5 6.3 fusion.185
  287.8 12.0 %multiply_convert_fusion.8 = (bf16[512,2048]{1,0:T(8,128)(2,1)}, bf16[512,2048]{1,0:T(8,128)(2,1)}, bf16[512,2048]{1,0:T(8,128)(2,1)}) fusion(f32[512,2048]{1,0:T(8,128)} %fusion.185, f32[512,2048]{1,0:T(8,128)S(1)} %fusion.186, bf16[512,2048]{1,0:T(8,128)(2,1)S(1)} %copy-done.35, bf16[2048,2048]{1,0:T(8,128)(2,1)} %param.25), kind=kOutput, calls=%fused_computation.118 | convolution fusion | flops 4310695936 | bytes 25165824 | tf_op jit(solution)/shard_map/dot_general | solution.py:56
  299.8 7.8 fusion.187
  307.6 9.4 add_convert_fusion.1
  317.4 69.4 %all-reduce.10.cloned.1.call-done = bf16[512,2048]{1,0:T(8,128)(2,1)} async-done(((bf16[512,2048]{1,0:T(8,128)(2,1)}), bf16[512,2048]{1,0:T(8,128)(2,1)}) %all-reduce.10.cloned.1.call-update) | async-done | bytes 2097168 | tf_op jit(solution)/shard_map/psum | solution.py:176
  421.2 5.5 fusion.108
  452.0 27.3 %multiply_reduce_fusion = (f32[512]{0:T(512)S(1)}, f32[512]{0:T(512)S(1)}, f32[512]{0:T(512)S(1)}, f32[512]{0:T(512)S(1)}, f32[512]{0:T(512)S(1)}, /*index=5*/f32[512,4096]{1,0:T(8,128)}) fusion(f32[512,4096]{1,0:T(8,128)} %get-tuple-element.138, f32[512]{0:T(512)S(1)} %log_add_fusion, s32[512]{0:T(512)S(1)} %copy-done.52, s32[4096]{0:T(1024)S(1)} %copy-done.49, ...), kind=kOutput, calls=%fused_computation.7 | convolution fusion | flops 316667392 | bytes 84516872 | tf_op jit(solution)/shard_map/while/body/eval_jaxpr/dot_general | solution.py:56
  479.3 26.9 %multiply_reduce_fusion.1 = (f32[512]{0:T(512)S(1)}, f32[512]{0:T(512)S(1)}, f32[512]{0:T(512)S(1)}, bf16[512,4096]{1,0:T(8,128)(2,1)}, f32[512,4096]{1,0:T(8,128)}) fusion(f32[512,4096]{1,0:T(8,128)} %get-tuple-element.136, f32[512]{0:T(512)S(1)} %get-tuple-element.145, s32[512]{0:T(512)S(1)} %copy-done.52, s32[4096]{0:T(1024)S(1)} %copy-done.49, ...), kind=kOutput, calls=%fused_computation.10 | convolution fusion | flops 310376960 | bytes 71929864 | tf_op jit(solution)/shard_map/while/body/eval_jaxpr/dot_general | solution.py:56
  506.2 21.4 %multiply_convert_fusion.2 = (bf16[512,4096]{1,0:T(8,128)(2,1)}, bf16[512,4096]{1,0:T(8,128)(2,1)}, bf16[512,4096]{1,0:T(8,128)(2,1)S(1)}) fusion(f32[512,4096]{1,0:T(8,128)} %fusion.86, f32[512]{0:T(512)S(1)} %get-tuple-element.88, f32[512,4096]{1,0:T(8,128)} %get-tuple-element.134, f32[512]{0:T(512)S(1)} %get-tuple-element.146, s32[512]{0:T(512)S(1)} %copy-done.52, ...), kind=kLoop, calls=%fused_computation.12 | loop fusion | flops 37748736 | bytes 62947328 | tf_op jit(solution)/shard_map/while/body/eval_jaxpr/convert_element_type | solution.py:204
  530.5 26.9 %multiply_convert_fusion.1 = (bf16[512,4096]{1,0:T(8,128)(2,1)}, bf16[512,4096]{1,0:T(8,128)(2,1)}, bf16[512,4096]{1,0:T(8,128)(2,1)}, bf16[512,4096]{1,0:T(8,128)(2,1)}) fusion(f32[512,4096]{1,0:T(8,128)} %get-tuple-element.140, f32[512]{0:T(512)S(1)} %get-tuple-element.74, f32[512,4096]{1,0:T(8,128)} %get-tuple-element.136, f32[512]{0:T(512)S(1)} %get-tuple-element.145, ...), kind=kLoop, calls=%fused_computation.9 | loop fusion | flops 48234496 | bytes 83922944 | tf_op jit(solution)/shard_map/while/body/eval_jaxpr/convert_element_type | solution.py:204
  596.6 11.1 reduce-scatter.9.cloned.1.call-done
  610.8 10.0 convolution_convert_fusion.5
  628.9 10.1 convolution_convert_fusion.1
  639.3 10.1 convolution_convert_fusion.2
  649.5 10.3 convolution_convert_fusion
  663.5 17.2 %reduce-scatter.11.cloned.1.call-done = bf16[256,512]{1,0:T(8,128)(2,1)} async-done(((bf16[2048,512]{1,0:T(8,128)(2,1)}), bf16[256,512]{1,0:T(8,128)(2,1)}) %reduce-scatter.11.cloned.1.call-update) | async-done | bytes 262160 | tf_op jit(solution)/shard_map/reduce_scatter | solution.py:249
  682.4 30.1 %reduce-scatter.13.cloned.1.call-done = bf16[256,128]{1,0:T(8,128)(2,1)} async-done(((bf16[2048,128]{1,0:T(8,128)(2,1)}), bf16[256,128]{1,0:T(8,128)(2,1)}) %reduce-scatter.13.cloned.1.call-update) | async-done | bytes 65552 | tf_op jit(solution)/shard_map/reduce_scatter | solution.py:252
  714.0 30.0 %reduce-scatter.15.cloned.1.call-done = bf16[256,128]{1,0:T(8,128)(2,1)} async-done(((bf16[2048,128]{1,0:T(8,128)(2,1)}), bf16[256,128]{1,0:T(8,128)(2,1)}) %reduce-scatter.15.cloned.1.call-update) | async-done | bytes 65552 | tf_op jit(solution)/shard_map/reduce_scatter | solution.py:255
  745.5 105.1 %all-reduce.12.cloned.1.call-done = (bf16[512,2048]{1,0:T(8,128)(2,1)}, bf16[512,2048]{1,0:T(8,128)(2,1)}) async-done(((bf16[512,2048]{1,0:T(8,128)(2,1)}, bf16[512,2048]{1,0:T(8,128)(2,1)}), (bf16[512,2048]{1,0:T(8,128)(2,1)}, bf16[512,2048]{1,0:T(8,128)(2,1)})) %all-reduce.12.cloned.1.call-update) | async-done | bytes 4194320 | tf_op jit(solution)/shard_map/psum | solution.py:174
  853.8 17.2 %all-reduce.2 = (bf16[2048]{0:T(1024)(128)(2,1)S(1)}, bf16[2048]{0:T(1024)(128)(2,1)S(1)}) all-reduce(bf16[2048]{0:T(1024)(128)(2,1)S(1)} %get-tuple-element.67, bf16[2048]{0:T(1024)(128)(2,1)S(1)} %copy-done.59), channel_id=3, replica_groups=mesh['wide'=8,'narrow'=4] {'wide'}, use_global_device_ids=true, to_apply=%region_38.39.clone | all-reduce | flops 4096 | bytes 16384
  881.1 62.1 %reduce-scatter.21.cloned.1.call-done = bf16[256,2048]{1,0:T(8,128)(2,1)} async-done(((bf16[2048,2048]{1,0:T(8,128)(2,1)}), bf16[256,2048]{1,0:T(8,128)(2,1)}) %reduce-scatter.21.cloned.1.call-update) | async-done | bytes 1048592 | tf_op jit(solution)/shard_map/reduce_scatter | solution.py:267
  946.0 87.3 %reduce-scatter.19.cloned.1.call-done = bf16[256,2048]{1,0:T(8,128)(2,1)} async-done(((bf16[2048,2048]{1,0:T(8,128)(2,1)}), bf16[256,2048]{1,0:T(8,128)(2,1)}) %reduce-scatter.19.cloned.1.call-update) | async-done | bytes 1048592 | tf_op jit(solution)/shard_map/reduce_scatter | solution.py:264
  1036.1 87.6 %reduce-scatter.23.cloned.1.call-done = bf16[2048,256]{1,0:T(8,128)(2,1)} async-done(((bf16[2048,2048]{1,0:T(8,128)(2,1)}), bf16[2048,256]{1,0:T(8,128)(2,1)}) %reduce-scatter.23.cloned.1.call-update) | async-done | bytes 1048592 | tf_op jit(solution)/shard_map/reduce_scatter | solution.py:270
  (365 shorter events, 252.3 us)
Async XLA Ops:
  7.2 154.8 %copy-start = (bf16[512,2048]{1,0:T(8,128)(2,1)S(1)}, bf16[512,2048]{1,0:T(8,128)(2,1)}, u32[]{:S(2)}) copy-start(bf16[512,2048]{1,0:T(8,128)(2,1)} %param.21) | copy-start | bytes 6291460
  7.2 260.9 %all-reduce.8.cloned.1.call-start = ((), (), s32[]{:S(2)}) async-start(), calls=%async_computation.8 | async-start | bytes 8388608 | tf_op jit(solution)/shard_map/psum | solution.py:155
  7.3 100.3 %copy-start.51 = (s32[512]{0:T(512)}, s32[512]{0:T(512)S(1)}, u32[]{:S(2)}) copy-start(s32[512]{0:T(512)S(1)} %iota_add_fusion) | copy-start | bytes 6148
  10.2 46.2 %copy-start.57 = (f32[512]{0:T(512)}, f32[512]{0:T(512)S(1)}, u32[]{:S(2)}) copy-start(f32[512]{0:T(512)S(1)} %get-tuple-element.120) | copy-start | bytes 6148
  11.9 95.7 %copy-start.55 = (s32[512]{0:T(512)}, s32[512]{0:T(512)S(1)}, u32[]{:S(2)}) copy-start(s32[512]{0:T(512)S(1)} %get-tuple-element.89) | copy-start | bytes 6148
  12.6 43.8 %copy-start.53 = (f32[2048]{0:T(1024)}, f32[2048]{0:T(1024)S(1)}, u32[]{:S(2)}) copy-start(f32[2048]{0:T(1024)S(1)} %convert_element_type.251) | copy-start | bytes 24580
  12.6 43.8 %copy-start.34 = (bf16[2048,512]{1,0:T(8,128)(2,1)S(1)}, bf16[2048,512]{1,0:T(8,128)(2,1)}, u32[]{:S(2)}) copy-start(bf16[2048,512]{1,0:T(8,128)(2,1)} %param.18) | copy-start | bytes 6291460
  17.3 41.2 %copy-start.36 = (f32[512,32]{0,1:T(8,128)}, f32[512,32]{0,1:T(8,128)S(1)}, u32[]{:S(2)}) copy-start(f32[512,32]{0,1:T(8,128)S(1)} %get-tuple-element.118) | copy-start | bytes 196612
  17.4 8.6 collective-permute-start
  26.0 7.6 collective-permute-start.1
  33.6 7.6 collective-permute-start.2
  41.2 7.6 collective-permute-start.3
  48.8 7.6 collective-permute-start.4
  56.3 7.7 collective-permute-start.5
  64.0 8.4 collective-permute-start.6
  65.9 41.8 %copy-start.48 = (s32[4096]{0:T(1024)}, s32[4096]{0:T(1024)S(1)}, u32[]{:S(2)}) copy-start(s32[4096]{0:T(1024)S(1)} %convert_reduce_fusion) | copy-start | bytes 49156
  67.0 40.7 %copy-start.31 = (bf16[512,8,2,32]{0,3,2,1:T(8,128)(2,1)}, bf16[512,8,2,32]{0,3,2,1:T(8,128)(2,1)S(1)}, u32[]{:S(2)}) copy-start(bf16[512,8,2,32]{0,3,2,1:T(8,128)(2,1)S(1)} %pad_maximum_fusion.1) | copy-start | bytes 1572868
  94.7 48.8 %copy-start.4 = (f32[512,4096]{1,0:T(8,128)}, f32[512,4096]{1,0:T(8,128)S(1)}, u32[]{:S(2)}) copy-start(f32[512,4096]{1,0:T(8,128)S(1)} %get-tuple-element.126) | copy-start | bytes 25165828
  97.3 49.3 %copy-start.5 = (f32[512,4096]{1,0:T(8,128)}, f32[512,4096]{1,0:T(8,128)S(1)}, u32[]{:S(2)}) copy-start(f32[512,4096]{1,0:T(8,128)S(1)} %get-tuple-element.128) | copy-start | bytes 25165828
  165.4 221.4 %all-reduce.10.cloned.1.call-start = ((), (), s32[]{:S(2)}) async-start(), calls=%async_computation.9 | async-start | bytes 4194304 | tf_op jit(solution)/shard_map/psum | solution.py:176
  317.0 290.6 %reduce-scatter.9.cloned.1.call-start = ((), (), s32[]{:S(2)}) async-start(), calls=%async_computation.10 | async-start | bytes 2359296 | tf_op jit(solution)/shard_map/reduce_scatter | solution.py:226
  571.7 90.0 %reduce-scatter.17.cloned.1.call-start = ((), (), s32[]{:S(2)}) async-start(), calls=%async_computation.14 | async-start | bytes 2359296 | tf_op jit(solution)/shard_map/reduce_scatter | solution.py:258
  576.6 104.1 %reduce-scatter.11.cloned.1.call-start = ((), (), s32[]{:S(2)}) async-start(), calls=%async_computation.11 | async-start | bytes 2359296 | tf_op jit(solution)/shard_map/reduce_scatter | solution.py:249
  596.5 116.0 %reduce-scatter.13.cloned.1.call-start = ((), (), s32[]{:S(2)}) async-start(), calls=%async_computation.12 | async-start | bytes 589824 | tf_op jit(solution)/shard_map/reduce_scatter | solution.py:252
  610.6 133.5 %reduce-scatter.15.cloned.1.call-start = ((), (), s32[]{:S(2)}) async-start(), calls=%async_computation.13 | async-start | bytes 589824 | tf_op jit(solution)/shard_map/reduce_scatter | solution.py:255
  622.7 227.9 %all-reduce.12.cloned.1.call-start = ((), (), s32[]{:S(2)}) async-start(), calls=%async_computation.18 | async-start | bytes 8388608 | tf_op jit(solution)/shard_map/psum | solution.py:174
  628.9 314.3 %reduce-scatter.21.cloned.1.call-start = ((), (), s32[]{:S(2)}) async-start(), calls=%async_computation.16 | async-start | bytes 9437184 | tf_op jit(solution)/shard_map/reduce_scatter | solution.py:267
  639.1 394.2 %reduce-scatter.19.cloned.1.call-start = ((), (), s32[]{:S(2)}) async-start(), calls=%async_computation.15 | async-start | bytes 9437184 | tf_op jit(solution)/shard_map/reduce_scatter | solution.py:264
  649.5 474.2 %reduce-scatter.23.cloned.1.call-start = ((), (), s32[]{:S(2)}) async-start(), calls=%async_computation.17 | async-start | bytes 9437184 | tf_op jit(solution)/shard_map/reduce_scatter | solution.py:270
  659.8 194.0 %copy-start.59 = (bf16[2048]{0:T(1024)(128)(2,1)S(1)}, bf16[2048]{0:T(1024)(128)(2,1)}, u32[]{:S(2)}) copy-start(bf16[2048]{0:T(1024)(128)(2,1)} %get-tuple-element.65) | copy-start | bytes 12292
  680.6 196.7 %copy-start.61 = (f32[512]{0:T(512)S(1)}, f32[512]{0:T(512)}, u32[]{:S(2)}) copy-start(f32[512]{0:T(512)} %get-tuple-element.119) | copy-start | bytes 6148
  878.5 247.9 %copy-start.1 = (bf16[512,2048]{1,0:T(8,128)(2,1)S(1)}, bf16[512,2048]{1,0:T(8,128)(2,1)}, u32[]{:S(2)}) copy-start(bf16[512,2048]{1,0:T(8,128)(2,1)} %param.21) | copy-start | bytes 6291460
  (82 other events, 485.6 us)
Sparse Core Ops, SparseCore 0:
  165.6 102.5 all-reduce.7
  317.1 69.6 all-reduce.9
  571.8 35.7 reduce-scatter.8
  609.8 34.3 reduce-scatter.16
  646.3 34.2 reduce-scatter.10
  682.7 29.7 reduce-scatter.12
  714.9 29.1 reduce-scatter.14
  748.1 102.4 all-reduce.11
  853.0 90.1 reduce-scatter.20
  945.4 87.7 reduce-scatter.18
  1035.7 87.9 reduce-scatter.22
